TPU v7x, 512 devices: a whole 4x8x8 slice. The times are simulated.
512 devices in a mesh: grp: 64 (over y, z), tp: 8 (over x, core).
Axes of the slice: x: 4, y: 8, z: 8, core: 2. Of those that a mesh axis runs over, the one named last changes fastest.
Arguments:
- normed_token_input: bfloat16 [65536, 4096], P('grp', 'tp'), may hold values from -6 to 6
- queries: bfloat16 [65536, 4096], P('grp', 'tp'), may hold values from -6 to 6
- fresh_token_keys: bfloat16 [65536, 1024], P('grp', 'tp'), may hold values from -6 to 6
- fresh_token_values: bfloat16 [65536, 1024], P('grp', 'tp'), may hold values from -6 to 6
- token_request_index: int32 [65536], P('grp'), may hold values from 0 to 255, never falling along the last dimension, each value on 1 to 1024 neighbouring positions
- prefix_page_cache: bfloat16 [128, 2, 128, 1024], P('grp', None, None, 'tp'), may hold values from -6 to 6
- adapter_down_weight: bfloat16 [128, 16, 4096], P('grp', None, 'tp'), may hold values from -0.09375 to 0.09375
- adapter_up_weight: bfloat16 [128, 16, 4096], P('grp', None, 'tp'), may hold values from -1.5 to 1.5
- group_page_list: int32 [64, 4], replicated, may hold values from 0 to 127, as said below
- group_adapter_list: int32 [64, 4], replicated, may hold values from 0 to 127, as said below
- page_entry_index: int32 [256], replicated, may hold values from 0 to 3
- adapter_entry_index: int32 [256], replicated, may hold values from 0 to 3
Outputs:
- attended: bfloat16 [65536, 4096], P('grp', 'tp')
Inputs may be any that keep to these rules, and one draw needn't show every extreme that they name: `group_page_list`: the 4 pages of a row lie with distinct owners: page // 2 differs within a row. `group_adapter_list`: the 4 adapters of a row lie with distinct owners: adapter // 2 differs within a row.
All inputs are finite; a program needn't handle non-finite values.
Results may differ from a plain program's by a relative error of at most 0.0065.
Values may be sent and summed in bfloat16 or wider, within the bound.
A program may use at most 64 MiB of HBM per device.

v0:
```python
import jax
import jax.numpy as jnp
from jax import lax
from jax.sharding import PartitionSpec as P

QUERY_HEADS = 32
KV_HEADS = 8
HEAD_WIDTH = 128
PAGE = 128


adapter_scale = 0.5


def passed_along(shard, axis, by):
    peers = lax.axis_size(axis)
    pairs = [(i, i + by) for i in range(peers) if 0 <= i + by < peers]
    return lax.ppermute(shard, axis, pairs)


def local(
    normed_token_input,
    queries,
    fresh_token_keys,
    fresh_token_values,
    token_request_index,
    prefix_page_cache,
    adapter_down_weight,
    adapter_up_weight,
    group_page_list,
    group_adapter_list,
    page_entry_index,
    adapter_entry_index,
):
    groups = lax.axis_size("grp")
    own_group = lax.axis_index("grp")
    tokens = queries.shape[0]
    adapters_used = group_adapter_list.shape[1]
    rank_width = adapter_down_weight.shape[1]
    key_width = fresh_token_keys.shape[1]
    head_dim = HEAD_WIDTH
    kv_local = key_width // head_dim
    heads_local = queries.shape[1] // head_dim
    per_kv = QUERY_HEADS // KV_HEADS
    group_pick = (jnp.arange(groups, dtype=jnp.int32) == own_group).astype(jnp.int32)
    page_row = jnp.sum(group_pick[:, None] * group_page_list, axis=0)
    adapter_entry_row = jnp.sum(group_pick[:, None] * group_adapter_list, axis=0)
    pieces = (
        lax.all_gather(prefix_page_cache, "grp", axis=0, tiled=True),
        lax.all_gather(adapter_down_weight, "grp", axis=0, tiled=True),
        lax.all_gather(adapter_up_weight, "grp", axis=0, tiled=True),
    )
    count = pieces[0].shape[0]
    stored = jnp.arange(count, dtype=jnp.int32)
    page_pick = (page_row[:, None] == stored[None, :]).astype(jnp.bfloat16)
    adapter_pick = (adapter_entry_row[:, None] == stored[None, :]).astype(jnp.bfloat16)
    pages = jnp.einsum(
        "pn,nabc->pabc", page_pick, pieces[0], preferred_element_type=jnp.float32
    ).astype(jnp.bfloat16)
    down_factors = jnp.einsum(
        "pn,nrd->prd", adapter_pick, pieces[1], preferred_element_type=jnp.float32
    ).astype(jnp.bfloat16)
    up_factors = jnp.einsum(
        "pn,nrd->prd", adapter_pick, pieces[2], preferred_element_type=jnp.float32
    ).astype(jnp.bfloat16)
    requests = jnp.arange(page_entry_index.shape[0], dtype=jnp.int32)
    member = (token_request_index[:, None] == requests[None, :]).astype(jnp.int32)
    page_of = jnp.sum(member * page_entry_index[None, :], axis=1)
    adapter_of = jnp.sum(member * adapter_entry_index[None, :], axis=1)
    adapter_mask = (
        adapter_of[:, None] == jnp.arange(adapters_used, dtype=jnp.int32)[None, :]
    ).astype(jnp.float32)
    expanded = jnp.repeat(adapter_mask, rank_width, axis=1)
    partial_terms = (
        jnp.einsum(
            "td,kd->tk",
            normed_token_input,
            down_factors.reshape(adapters_used * rank_width, -1),
            preferred_element_type=jnp.float32,
        )
        * expanded
    )
    summed = lax.psum(partial_terms, "tp")
    lowrank = summed.astype(jnp.bfloat16)
    query_update = jnp.dot(
        lowrank,
        up_factors.reshape(adapters_used * rank_width, -1),
        preferred_element_type=jnp.float32,
    )
    query_adapted = (queries.astype(jnp.float32) + adapter_scale * query_update).astype(
        jnp.bfloat16
    )
    stacked = jnp.stack([fresh_token_keys, fresh_token_values])
    before = passed_along(stacked, "grp", 1)
    before_ids = passed_along(token_request_index + 1, "grp", 1)
    page_keys = pages[:, 0].reshape(-1, key_width)
    page_values = pages[:, 1].reshape(-1, key_width)
    keys_all = (
        jnp.concatenate([page_keys, before[0], fresh_token_keys], 0)
        .reshape(-1, kv_local, head_dim)
        .transpose(1, 0, 2)
    )
    values_all = (
        jnp.concatenate([page_values, before[1], fresh_token_values], 0)
        .reshape(-1, kv_local, head_dim)
        .transpose(1, 0, 2)
    )
    page_cols = jnp.arange(page_keys.shape[0], dtype=jnp.int32) // PAGE
    see_page = page_of[:, None] == page_cols[None, :]
    see_prev = before_ids[None, :] == token_request_index[:, None] + 1
    order = jnp.arange(tokens, dtype=jnp.int32)
    see_own = (token_request_index[None, :] == token_request_index[:, None]) & (
        order[None, :] <= order[:, None]
    )
    visible = jnp.concatenate([see_page, see_prev, see_own], 1)
    block = min(512, tokens)
    nblocks = tokens // block
    query_three = query_adapted.reshape(tokens, heads_local, head_dim)

    def one_block(counter):
        head = counter // nblocks
        first_row = counter % nblocks * block
        rows = lax.dynamic_slice_in_dim(query_three, first_row, block, 0)
        query_head = lax.dynamic_index_in_dim(rows, head, 1, keepdims=False)
        key_head = lax.dynamic_index_in_dim(keys_all, head // per_kv, 0, keepdims=False)
        value_head = lax.dynamic_index_in_dim(values_all, head // per_kv, 0, keepdims=False)
        sight = lax.dynamic_slice_in_dim(visible, first_row, block, 0)
        scores = jnp.einsum("qd,kd->qk", query_head, key_head, preferred_element_type=jnp.float32)
        scores = jnp.where(sight, scores * HEAD_WIDTH ** (-0.5), jnp.float32(-1e30))
        highest = jnp.max(scores, axis=1, keepdims=True)
        expo = jnp.where(sight, jnp.exp(scores - highest), jnp.float32(0.0))
        weights = (expo / jnp.sum(expo, axis=1, keepdims=True)).astype(jnp.bfloat16)
        return jnp.dot(weights, value_head, preferred_element_type=jnp.float32).astype(jnp.bfloat16)

    outputs = lax.map(one_block, jnp.arange(heads_local * nblocks, dtype=jnp.int32))
    return (
        outputs.reshape(heads_local, tokens, head_dim)
        .transpose(1, 0, 2)
        .reshape(tokens, heads_local * head_dim)
    )


def solution(mesh):
    placed = (
        P("grp", "tp"),
        P("grp", "tp"),
        P("grp", "tp"),
        P("grp", "tp"),
        P("grp"),
        P("grp", None, None, "tp"),
        P("grp", None, "tp"),
        P("grp", None, "tp"),
        P(),
        P(),
        P(),
        P(),
    )
    return jax.shard_map(
        local, mesh=mesh, in_specs=placed, out_specs=P("grp", "tp"), check_vma=False
    )
```

profile of v0, /device:TPU:6, one launch (start us, length us, event | category | flops | bytes accessed | tf_op | source)
XLA Modules:
  0.0 371.7 jit_solution(2571474612851178525)
XLA Ops:
  8.7 1.9 pad_maximum_fusion
  10.6 5.1 %collective-permute-start.1 = (bf16[2,1024,128]{2,1,0:T(8,128)(2,1)}, bf16[2,1024,128]{2,1,0:T(8,128)(2,1)}, u32[]{:S(2)}, u32[]{:S(2)}) collective-permute-start(bf16[2,1024,128]{2,1,0:T(8,128)(2,1)} %pad_maximum_fusion), channel_id=1, source_target_pairs={{0,8},{8,16},{16,24},{24,32},{32,40},{40,48},{48,56},{56,64},{64,7... | collective-permute-start | bytes 1572872 | tf_op jit(solution)/shard_map/ppermute | solution.py:18
  16.4 3.5 collective-permute-start
  27.1 2.6 pad_add_fusion
  30.8 67.9 %all-gather.4.cloned.1.call-done = bf16[128,16,512]{2,1,0:T(8,128)(2,1)} async-done(((bf16[2,16,512]{2,1,0:T(8,128)(2,1)}), bf16[128,16,512]{2,1,0:T(8,128)(2,1)}) %all-gather.4.cloned.1.call-update) | async-done | bytes 2097168 | tf_op jit(solution)/shard_map/all_gather | solution.py:50
  98.8 3.9 %fusion.23 = bf16[4,16,512]{2,0,1:T(4,128)(2,1)S(1)} fusion(bf16[128,16,512]{2,1,0:T(8,128)(2,1)} %all-gather.4.cloned.1.call-done, s32[4]{0:T(128)S(1)} %get-tuple-element.158), kind=kOutput, calls=%fused_computation.29 | convolution fusion | flops 8421888 | bytes 2162704 | tf_op jit(solution)/shard_map/pn,nrd->prd/dot_general | solution.py:60
  103.1 79.2 %all-gather.6.cloned.1.call-done = bf16[128,16,512]{2,1,0:T(8,128)(2,1)} async-done(((bf16[2,16,512]{2,1,0:T(8,128)(2,1)}), bf16[128,16,512]{2,1,0:T(8,128)(2,1)}) %all-gather.6.cloned.1.call-update) | async-done | bytes 2097168 | tf_op jit(solution)/shard_map/all_gather | solution.py:51
  182.3 3.9 %fusion.26 = bf16[4,16,512]{2,0,1:T(4,128)(2,1)S(1)} fusion(bf16[128,16,512]{2,1,0:T(8,128)(2,1)} %all-gather.6.cloned.1.call-done, s32[4]{0:T(128)S(1)} %get-tuple-element.158), kind=kOutput, calls=%fused_computation.30 | convolution fusion | flops 8421888 | bytes 2162704 | tf_op jit(solution)/shard_map/pn,nrd->prd/dot_general | solution.py:63
  186.2 23.4 %all-reduce.1 = bf16[1024,64]{0,1:T(8,128)(2,1)S(1)} all-reduce(f32[1024,64]{0,1:T(8,128)S(1)} %fusion.22), channel_id=1, replica_groups=mesh['grp'=64,'tp'=8] {'tp'}, use_global_device_ids=true, to_apply=%region_2.0 | all-reduce | flops 65536 | bytes 393216 | tf_op jit(solution)/shard_map/psum | solution.py:83
  211.2 70.4 %all-gather.8.cloned.1.call-done = bf16[128,2,128,128]{3,2,1,0:T(8,128)(2,1)} async-done(((bf16[2,2,128,128]{3,2,1,0:T(8,128)(2,1)}), bf16[128,2,128,128]{3,2,1,0:T(8,128)(2,1)}) %all-gather.8.cloned.1.call-update) | async-done | bytes 8388624 | tf_op jit(solution)/shard_map/all_gather | solution.py:49
  281.5 8.0 %fusion.19 = bf16[4,2,128,128]{3,0,2,1:T(4,128)(2,1)S(1)} fusion(bf16[128,2,128,128]{3,2,1,0:T(8,128)(2,1)} %all-gather.8.cloned.1.call-done, s32[4]{0:T(128)S(1)} %get-tuple-element.157), kind=kOutput, calls=%fused_computation.26 | convolution fusion | flops 33686016 | bytes 8650768 | tf_op jit(solution)/shard_map/pn,nabc->pabc/dot_general | solution.py:57
  290.8 72.3 %while.13 = (s32[]{:T(128)}, bf16[8,512,128]{2,1,0:T(8,128)(2,1)S(1)}, s32[8]{0:T(128)S(1)}, pred[1024,2560]{1,0:T(32,128)(4,1)}, bf16[1024,4,128]{0,2,1:T(8,128...) while((s32[]{:T(128)}, ...), condition=%wide.region_8.9_spmd, body=%wide.region_5.8_spmd.sunk | while | flops 684260352 | bytes 34351636 | solution.py:135
  294.0 2.9 fusion.53
  303.1 2.9 fusion.53
  307.4 1.5 fusion.55
  312.1 2.9 fusion.53
  316.4 1.5 fusion.55
  321.2 2.9 fusion.53
  325.5 1.5 fusion.55
  330.2 3.0 fusion.53
  334.5 1.5 fusion.55
  339.3 2.9 fusion.53
  348.3 3.0 fusion.53
  357.4 2.9 fusion.53
  (96 shorter events, 37.7 us)
Async XLA Ops:
  6.5 96.2 %copy-start = (bf16[1024,512]{1,0:T(8,128)(2,1)S(1)}, bf16[1024,512]{1,0:T(8,128)(2,1)}, u32[]{:S(2)}) copy-start(bf16[1024,512]{1,0:T(8,128)(2,1)} %param.14) | copy-start | bytes 3145732
  6.5 17.2 %copy-start.6 = (s32[64,4]{0,1:T(4,128)S(1)}, s32[64,4]{0,1:T(4,128)}, u32[]{:S(2)}) copy-start(s32[64,4]{0,1:T(4,128)} %param.22) | copy-start | bytes 3076
  6.5 17.2 %copy-start.7 = (s32[64,4]{0,1:T(4,128)S(1)}, s32[64,4]{0,1:T(4,128)}, u32[]{:S(2)}) copy-start(s32[64,4]{0,1:T(4,128)} %param.23) | copy-start | bytes 3076
  6.5 92.2 %all-gather.4.cloned.1.call-start = ((), (), s32[]{:S(2)}) async-start(), calls=%async_computation | async-start | bytes 2129920 | tf_op jit(solution)/shard_map/all_gather | solution.py:50
  7.3 175.1 %all-gather.6.cloned.1.call-start = ((), (), s32[]{:S(2)}) async-start(), calls=%async_computation.1 | async-start | bytes 2129920 | tf_op jit(solution)/shard_map/all_gather | solution.py:51
  8.0 273.5 %all-gather.8.cloned.1.call-start = ((), (), s32[]{:S(2)}) async-start(), calls=%async_computation.2 | async-start | bytes 8519680 | tf_op jit(solution)/shard_map/all_gather | solution.py:49
  10.6 19.1 %collective-permute-start.1 = (bf16[2,1024,128]{2,1,0:T(8,128)(2,1)}, bf16[2,1024,128]{2,1,0:T(8,128)(2,1)}, u32[]{:S(2)}, u32[]{:S(2)}) collective-permute-start(bf16[2,1024,128]{2,1,0:T(8,128)(2,1)} %pad_maximum_fusion), channel_id=1, source_target_pairs={{0,8},{8,16},{16,24},{24,32},{32,40},{40,48},{48,56},{56,64},{64,7... | collective-permute-start | bytes 1572872 | tf_op jit(solution)/shard_map/ppermute | solution.py:18
  16.4 10.0 %collective-permute-start = (s32[1024]{0:T(1024)S(1)}, s32[1024]{0:T(1024)S(1)}, u32[]{:S(2)}, u32[]{:S(2)}) collective-permute-start(s32[1024]{0:T(1024)S(1)} %broadcast_add_fusion), channel_id=1, source_target_pairs={{0,8},{8,16},{16,24},{24,32},{32,40},{40,48},{48,56},{56,64},{64,7... | collective-permute-start | bytes 12296 | tf_op jit(solution)/shard_map/ppermute | solution.py:18
  281.5 8.1 %copy-start.3 = (bf16[1024,128]{1,0:T(8,128)(2,1)S(1)}, bf16[1024,128]{1,0:T(8,128)(2,1)}, u32[]{:S(2)}) copy-start(bf16[1024,128]{1,0:T(8,128)(2,1)} %param.16) | copy-start | bytes 786436
  281.5 8.1 %copy-start.4 = (bf16[1024,128]{1,0:T(8,128)(2,1)S(1)}, bf16[1024,128]{1,0:T(8,128)(2,1)}, u32[]{:S(2)}) copy-start(bf16[1024,128]{1,0:T(8,128)(2,1)} %param.17) | copy-start | bytes 786436
  294.0 3.0 copy-start.1
  297.0 1.3 copy-start.5
  303.1 3.0 copy-start.1
  306.0 1.3 copy-start.5
  312.1 3.0 copy-start.1
  315.1 1.3 copy-start.5
  321.2 2.9 copy-start.1
  324.1 1.3 copy-start.5
  330.2 3.0 copy-start.1
  333.2 1.3 copy-start.5
  339.3 2.9 copy-start.1
  342.2 1.3 copy-start.5
  348.3 3.0 copy-start.1
  357.3 2.9 copy-start.1
  (3 other events, 4.0 us)
Sparse Core Ops, SparseCore 0:
  10.4 88.3 all-gather.3
  101.8 80.5 all-gather.5
  185.4 96.1 all-gather.7
where the time goes:
time: 373 us; the launch traced here: 372 us
  waiting for transfers between devices  221 us (59%)
  matrix products  53.3 us (14%)
  blocking collectives  23.4 us (6%)
  other arithmetic  21.3 us (6%)
  loops' own time  21.3 us (6%)
  between operations  13.3 us (4%)
  local copies, waits for them, and re-layouts  9.69 us (3%)
  starting transfers between devices  8.62 us (2%)
    all_gather x1, waiting for transfers between devices, local(): lax.all_gather(adapter_up_weight, 'grp', axis=0, tiled=True)  79.2 us
    all_gather x1, waiting for transfers between devices, local(): lax.all_gather(prefix_page_cache, 'grp', axis=0, tiled=True)  70.4 us
    all_gather x1, waiting for transfers between devices, local(): lax.all_gather(adapter_down_weight, 'grp', axis=0, tiled=True)  67.9 us
    dot_general x8, matrix products, one_block(): jnp.einsum('qd,kd->qk', query_head, key_head, preferred_element_type=jnp....  23.5 us
    psum x1, blocking collectives, local(): summed = lax.psum(partial_terms, 'tp')  23.4 us
    another operation x1, loops' own time, local(): lax.map(one_block, jnp.arange(heads_local * nblocks, dtype=jnp.int32))  21.3 us
    dot_general x8, matrix products, one_block(): jnp.dot(weights, value_head, preferred_element_type=jnp.float32)  12.1 us
    reduce_sum x8, other arithmetic, one_block(): weights = (expo / jnp.sum(expo, axis=1, keepdims=True)).astype(jnp.bfloat16)  10.6 us
  transfers between devices with their start and end apart: 5, of which 4 were waited for; matrix products, arithmetic and copies ran while one was open for 6% of the time, Pallas kernels for 0%

commit v1 on v0

v1 whole, which is shorter than its diff:
```python
import functools
import math

import jax
import jax.numpy as jnp
from jax import lax
from jax.experimental import pallas as pl
from jax.experimental.pallas import tpu as pltpu
from jax.sharding import PartitionSpec as P

PER_KV = 4
HEAD_WIDTH = 128
PAGE = 128
BLOCK = 128
ADAPTER_SCALE = 0.5
MESH = pl.DeviceIdType.MESH
F32 = jnp.float32
BF16 = jnp.bfloat16


def ring_split(n, heavy_right):
    more, fewer = n // 2, (n - 1) // 2
    return (more, fewer) if heavy_right else (fewer, more)


def token_codes(ids_row, table_columns):
    requests = table_columns.shape[0]
    numbers = lax.broadcasted_iota(jnp.int32, (requests, ids_row.shape[1]), 0)
    return jnp.sum(jnp.where(numbers == ids_row, table_columns, 0), axis=0, keepdims=True)


def as_columns(row):
    return jnp.broadcast_to(row, (128, row.shape[1])).T


class Gather:
    def __init__(self, table, pos, n, right_id, left_id, split, send, recv):
        self.rights, self.lefts = split
        self.copies = []
        for s in range(1, max(split) + 1):
            now = []
            for way, (count, peer) in enumerate(((self.rights, right_id), (self.lefts, left_id))):
                if s <= count:
                    origin = lax.rem(pos - (s - 1) + n, n) if way == 0 else lax.rem(pos + (s - 1), n)
                    at = s - 1 if way == 0 else self.rights + s - 1
                    now.append(
                        pltpu.make_async_remote_copy(
                            src_ref=table.at[origin],
                            dst_ref=table.at[origin],
                            send_sem=send.at[at],
                            recv_sem=recv.at[at],
                            device_id=peer,
                            device_id_type=MESH,
                        )
                    )
                else:
                    now.append(None)
            self.copies.append(now)
        self.steps = len(self.copies)

    def start(self, s):
        for copy in self.copies[s]:
            if copy is not None:
                copy.start()

    def forward(self, s):
        for way, copy in enumerate(self.copies[s]):
            if copy is not None:
                copy.wait_recv()
                if s + 1 < self.steps and self.copies[s + 1][way] is not None:
                    self.copies[s + 1][way].start()

    def finish(self):
        for now in self.copies:
            for copy in now:
                if copy is not None:
                    copy.wait_send()


class Slots:
    def __init__(self, table, lists, slots, pos, n, right_id, left_id, split, send, recv, group_at, index_of, place_of):
        self.table, self.lists, self.slots, self.pos, self.n = table, lists, slots, pos, n
        self.split = split
        self.group_at, self.index_of, self.place_of = group_at, index_of, place_of
        self.copies = []
        for way, (count, peer) in enumerate(((split[0], right_id), (split[1], left_id))):
            base = 0 if way == 0 else split[0] + 1
            sems = 0 if way == 0 else split[0]
            self.copies.append(
                [
                    pltpu.make_async_remote_copy(
                        src_ref=slots.at[base + s],
                        dst_ref=slots.at[base + s + 1],
                        send_sem=send.at[sems + s],
                        recv_sem=recv.at[sems + s],
                        device_id=peer,
                        device_id_type=MESH,
                    )
                    for s in range(count)
                ]
            )
        self.steps = max(split)

    def fill(self, way, s):
        count = self.split[way]
        base = 0 if way == 0 else self.split[0] + 1
        away = count - s
        target = lax.rem(self.pos + away, self.n) if way == 0 else lax.rem(self.pos - away + self.n, self.n)
        group = self.group_at(target)
        for k in range(self.lists.shape[1]):
            item = self.lists[group, k]
            mine = self.table[self.index_of(item)]
            if s > 0:
                mine = jnp.where(self.place_of(item) == self.pos, mine, self.slots[base + s, k])
            self.slots[base + s, k] = mine

    def start(self):
        for way in (0, 1):
            if self.split[way] > 0:
                self.fill(way, 0)
                self.copies[way][0].start()

    def forward(self, s):
        for way in (0, 1):
            count = self.split[way]
            if s < count:
                self.copies[way][s].wait_recv()
                if s + 1 < count:
                    self.fill(way, s + 1)
                    self.copies[way][s + 1].start()

    def entry(self, k):
        rights, lefts = self.split
        item = self.lists[self.group_at(self.pos), k]
        value = self.table[self.index_of(item)]
        ahead = lax.rem(self.place_of(item) - self.pos + self.n, self.n)
        if rights > 0:
            value = jnp.where(ahead > lefts, self.slots[rights, k], value)
        if lefts > 0:
            value = jnp.where((ahead > 0) & (ahead <= lefts), self.slots[rights + 1 + lefts, k], value)
        return value

    def finish(self):
        for way in (0, 1):
            for copy in self.copies[way]:
                copy.wait_send()


def fetch_kernel(
    ny, nz, ntp,
    page_list, adapter_list, ids_ref, entries_ref, x_ref, k_ref, v_ref, cache_ref, down_ref, up_ref,
    lowrank_ref, up_out, kpage_out, vpage_out, kprev_out, vprev_out, code_out, idprev_out,
    down_tab, up_tab, kpage_tab, vpage_tab,
    down_slots, up_slots, kpage_slots, vpage_slots,
    down_all, parts, arrived,
    gather_send, gather_recv, slot_send, slot_recv, prev_send, prev_recv, sum_send, sum_recv, all_send, all_recv,
):
    group = lax.axis_index("grp")
    tp = lax.axis_index("tp")
    groups = ny * nz
    y, z = lax.div(group, nz), lax.rem(group, nz)
    z_right = (y * nz + lax.rem(z + 1, nz), tp)
    z_left = (y * nz + lax.rem(z + nz - 1, nz), tp)
    y_right = (lax.rem(y + 1, ny) * nz + z, tp)
    y_left = (lax.rem(y + ny - 1, ny) * nz + z, tp)
    after = (lax.rem(group + 1, groups), tp)
    before = (lax.rem(group + groups - 1, groups), tp)

    barrier = pltpu.get_barrier_semaphore()
    others = [(group, lax.rem(tp + d, ntp)) for d in range(1, ntp)]
    greeted = [z_right, z_left, y_right, y_left, after, before] + others
    for peer in greeted:
        pl.semaphore_signal(barrier, inc=1, device_id=peer, device_id_type=MESH)

    stored = down_ref.shape[0]
    for n in range(stored):
        down_tab[z, n] = down_ref[n]
        up_tab[y, n] = up_ref[n]
        kpage_tab[z, n] = cache_ref[n, 0]
        vpage_tab[y, n] = cache_ref[n, 1]

    pl.semaphore_wait(barrier, len(greeted))

    zs, ys = ring_split(nz, False), ring_split(ny, True)
    gathers = [
        Gather(down_tab, z, nz, z_right, z_left, zs, gather_send.at[0], gather_recv.at[0]),
        Gather(up_tab, y, ny, y_right, y_left, ys, gather_send.at[1], gather_recv.at[1]),
        Gather(kpage_tab, z, nz, z_right, z_left, zs, gather_send.at[2], gather_recv.at[2]),
        Gather(vpage_tab, y, ny, y_right, y_left, ys, gather_send.at[3], gather_recv.at[3]),
    ]

    def along_y(table, lists, slots, at):
        return Slots(
            table, lists, slots, y, ny, y_right, y_left, ys, slot_send.at[at], slot_recv.at[at],
            lambda target: target * nz + z,
            lambda item: (lax.rem(lax.div(item, stored), nz), lax.rem(item, stored)),
            lambda item: lax.div(item, stored * nz),
        )

    def along_z(table, lists, slots, at):
        return Slots(
            table, lists, slots, z, nz, z_right, z_left, zs, slot_send.at[at], slot_recv.at[at],
            lambda target: y * nz + target,
            lambda item: (lax.div(item, stored * nz), lax.rem(item, stored)),
            lambda item: lax.rem(lax.div(item, stored), nz),
        )

    adapters = [along_y(down_tab, adapter_list, down_slots, 0), along_z(up_tab, adapter_list, up_slots, 1)]
    pages = [along_y(kpage_tab, page_list, kpage_slots, 2), along_z(vpage_tab, page_list, vpage_slots, 3)]

    def prev_copy(src, dst, at):
        return pltpu.make_async_remote_copy(
            src_ref=src, dst_ref=dst, send_sem=prev_send.at[at], recv_sem=prev_recv.at[at],
            device_id=after, device_id_type=MESH,
        )

    prevs = [prev_copy(ids_ref, idprev_out, 0), prev_copy(k_ref, kprev_out, 1), prev_copy(v_ref, vprev_out, 2)]

    for gather in gathers:
        gather.start(0)
    for copy in prevs:
        copy.start()

    chunks = ids_ref.shape[0]
    code_columns = as_columns(entries_ref[...])
    for c in range(chunks):
        code_out[pl.ds(c, 1), :] = token_codes(ids_ref[pl.ds(c, 1), :], code_columns)

    for s in range(max(g.steps for g in gathers)):
        for gather in gathers:
            if s < gather.steps:
                gather.forward(s)

    for ring in adapters + pages:
        ring.start()
    for s in range(max(ring.steps for ring in adapters)):
        for ring in adapters:
            if s < ring.steps:
                ring.forward(s)
        if s == 0:
            for ring in pages:
                ring.forward(0)

    rank = down_ref.shape[1]
    listed = adapter_list.shape[1]
    for k in range(listed):
        down_all[k * rank:(k + 1) * rank, :] = adapters[0].entry(k)
        up_out[k] = adapters[1].entry(k)
    partial = lax.dot_general(
        down_all[...], x_ref[...], (((1,), (1,)), ((), ())), preferred_element_type=F32
    )
    for c in range(chunks):
        entry = lax.rem(code_out[pl.ds(c, 1), :], listed)
        total = jnp.zeros((rank, BLOCK), F32)
        for k in range(listed):
            total = jnp.where(entry == k, partial[k * rank:(k + 1) * rank, c * BLOCK:(c + 1) * BLOCK], total)
        parts[c] = total

    each = chunks // ntp
    sums = []
    for d in range(1, ntp):
        peer = lax.rem(tp + d, ntp)
        copy = pltpu.make_async_remote_copy(
            src_ref=parts.at[pl.ds(peer * each, each)], dst_ref=arrived.at[d - 1],
            send_sem=sum_send.at[d - 1], recv_sem=sum_recv.at[d - 1],
            device_id=(group, peer), device_id_type=MESH,
        )
        copy.start()
        sums.append(copy)

    for ring in pages:
        if ring.steps > 1:
            ring.forward(1)

    total = parts[pl.ds(tp * each, each)]
    for d, copy in enumerate(sums):
        copy.wait_recv()
        total = total + arrived[d]
    lowrank_ref[pl.ds(tp * each, each)] = total.astype(BF16)
    spread = []
    for d in range(1, ntp):
        copy = pltpu.make_async_remote_copy(
            src_ref=lowrank_ref.at[pl.ds(tp * each, each)], dst_ref=lowrank_ref.at[pl.ds(tp * each, each)],
            send_sem=all_send.at[d - 1], recv_sem=all_recv.at[d - 1],
            device_id=(group, lax.rem(tp + d, ntp)), device_id_type=MESH,
        )
        copy.start()
        spread.append(copy)

    for s in range(2, max(ring.steps for ring in pages)):
        for ring in pages:
            if s < ring.steps:
                ring.forward(s)
    for k in range(page_list.shape[1]):
        kpage_out[pl.ds(k * PAGE, PAGE), :] = pages[0].entry(k)
        vpage_out[pl.ds(k * PAGE, PAGE), :] = pages[1].entry(k)

    for copy in spread + prevs:
        copy.wait_recv()
    for copy in sums + spread + prevs:
        copy.wait_send()
    for ring in gathers + adapters + pages:
        ring.finish()


def attend_kernel(
    q_ref, lowrank_ref, up_ref, kpage_ref, vpage_ref, kprev_ref, vprev_ref, k_ref, v_ref, code_ref, ids_ref, idprev_ref,
    out_ref, keys, values, key_ids,
):
    i = pl.program_id(0)
    tokens = k_ref.shape[0]
    chunks = tokens // BLOCK

    @pl.when(i == 0)
    def _():
        first = lax.axis_index("grp") == 0
        keys[:tokens, :] = kprev_ref[...]
        keys[tokens:, :] = k_ref[...]
        values[:tokens, :] = vprev_ref[...]
        values[tokens:, :] = v_ref[...]
        key_ids[:chunks, :] = jnp.where(first, -1, idprev_ref[...])
        key_ids[chunks:, :] = ids_ref[...]

    listed = up_ref.shape[0]
    code = code_ref[pl.ds(i, 1), :]
    entry = lax.rem(code, listed)
    low = lowrank_ref[0]
    wide = jnp.concatenate([jnp.where(entry == k, low, jnp.zeros_like(low)) for k in range(listed)], axis=0)
    up_all = jnp.concatenate([up_ref[k] for k in range(listed)], axis=0)
    update = lax.dot_general(wide, up_all, (((0,), (0,)), ((), ())), preferred_element_type=F32)
    query = (q_ref[...].astype(F32) + ADAPTER_SCALE * update).astype(BF16)

    page_of = as_columns(lax.div(code, listed))
    ids = as_columns(ids_ref[pl.ds(i, 1), :])
    start = pl.multiple_of(i * BLOCK, BLOCK)
    band = tokens + BLOCK
    kband = keys[pl.ds(start, band), :]
    vband = values[pl.ds(start, band), :]
    row = lax.broadcasted_iota(jnp.int32, (BLOCK, BLOCK), 0)
    column = lax.broadcasted_iota(jnp.int32, (BLOCK, BLOCK), 1)
    masks = []
    for c in range(chunks + 1):
        mask = ids == key_ids[pl.ds(i + c, 1), :]
        if c == chunks:
            mask = mask & (column <= row)
        masks.append(mask)
    npages = kpage_ref.shape[0] // PAGE
    for k in range(npages):
        masks.append(page_of == k)
    factor = math.log2(math.e) * HEAD_WIDTH ** -0.5
    nt = (((1,), (1,)), ((), ()))
    for h in range(PER_KV):
        qh = query[:, h * HEAD_WIDTH:(h + 1) * HEAD_WIDTH]
        sb = lax.dot_general(qh, kband, nt, preferred_element_type=F32)
        sp = lax.dot_general(qh, kpage_ref[...], nt, preferred_element_type=F32)
        pieces = [sb[:, c * BLOCK:(c + 1) * BLOCK] for c in range(chunks + 1)]
        pieces += [sp[:, c * PAGE:(c + 1) * PAGE] for c in range(npages)]
        pieces = [jnp.where(mask, piece, F32(-1e30)) for mask, piece in zip(masks, pieces)]
        top = functools.reduce(jnp.maximum, pieces)
        top = jnp.max(top, axis=1, keepdims=True)
        expos = [jnp.exp2((piece - top) * factor) for piece in pieces]
        total = jnp.sum(functools.reduce(jnp.add, expos), axis=1, keepdims=True)
        weights = [e.astype(BF16) for e in expos]
        mixed = jnp.dot(jnp.concatenate(weights[:chunks + 1], axis=1), vband, preferred_element_type=F32)
        mixed += jnp.dot(jnp.concatenate(weights[chunks + 1:], axis=1), vpage_ref[...], preferred_element_type=F32)
        out_ref[:, h * HEAD_WIDTH:(h + 1) * HEAD_WIDTH] = (mixed / total).astype(BF16)


def fetch(ny, nz, ntp, page_list, adapter_list, ids, entries, x, k, v, cache, down, up):
    chunks = ids.shape[0]
    stored, rank, features = down.shape
    listed, plisted = adapter_list.shape[1], page_list.shape[1]
    page_rows = plisted * PAGE
    struct = jax.ShapeDtypeStruct
    vmem = pl.BlockSpec(memory_space=pltpu.VMEM)
    smem = pl.BlockSpec(memory_space=pltpu.SMEM)
    anywhere = pl.BlockSpec(memory_space=pl.ANY)
    most = max(ny, nz) - 1
    each = chunks // ntp
    dma = pltpu.SemaphoreType.DMA
    return pl.pallas_call(
        functools.partial(fetch_kernel, ny, nz, ntp),
        out_shape=(
            struct((chunks, rank, BLOCK), BF16),
            struct((listed, rank, features), BF16),
            struct((page_rows, HEAD_WIDTH), BF16),
            struct((page_rows, HEAD_WIDTH), BF16),
            struct(k.shape, BF16),
            struct(v.shape, BF16),
            struct(ids.shape, jnp.int32),
            struct(ids.shape, jnp.int32),
        ),
        in_specs=[smem, smem, vmem, vmem, vmem, vmem, vmem, vmem, vmem, vmem],
        out_specs=(vmem,) * 8,
        scratch_shapes=[
            pltpu.VMEM((nz, stored, rank, features), BF16),
            pltpu.VMEM((ny, stored, rank, features), BF16),
            pltpu.VMEM((nz, stored, PAGE, HEAD_WIDTH), BF16),
            pltpu.VMEM((ny, stored, PAGE, HEAD_WIDTH), BF16),
            pltpu.VMEM((ny + 1, listed, rank, features), BF16),
            pltpu.VMEM((nz + 1, listed, rank, features), BF16),
            pltpu.VMEM((ny + 1, plisted, PAGE, HEAD_WIDTH), BF16),
            pltpu.VMEM((nz + 1, plisted, PAGE, HEAD_WIDTH), BF16),
            pltpu.VMEM((listed * rank, features), BF16),
            pltpu.VMEM((chunks, rank, BLOCK), F32),
            pltpu.VMEM((max(ntp - 1, 1), each, rank, BLOCK), F32),
            dma((4, most)), dma((4, most)), dma((4, most)), dma((4, most)),
            dma((3,)), dma((3,)),
            dma((max(ntp - 1, 1),)), dma((max(ntp - 1, 1),)), dma((max(ntp - 1, 1),)), dma((max(ntp - 1, 1),)),
        ],
        compiler_params=pltpu.CompilerParams(
            collective_id=0, has_side_effects=True, vmem_limit_bytes=40 * 1024 * 1024
        ),
        name="fetch",
    )(page_list, adapter_list, ids, entries, x, k, v, cache, down, up)


def attend(q, lowrank, up, kpage, vpage, kprev, vprev, k, v, code, ids, idprev):
    tokens, width = q.shape
    rank = lowrank.shape[1]
    whole = lambda a: pl.BlockSpec(a.shape, lambda i: (0,) * a.ndim)
    return pl.pallas_call(
        attend_kernel,
        grid=(tokens // BLOCK,),
        out_shape=jax.ShapeDtypeStruct(q.shape, BF16),
        in_specs=[
            pl.BlockSpec((BLOCK, width), lambda i: (i, 0)),
            pl.BlockSpec((1, rank, BLOCK), lambda i: (i, 0, 0)),
        ] + [whole(a) for a in (up, kpage, vpage, kprev, vprev, k, v, code, ids, idprev)],
        out_specs=pl.BlockSpec((BLOCK, width), lambda i: (i, 0)),
        scratch_shapes=[
            pltpu.VMEM((2 * tokens, HEAD_WIDTH), BF16),
            pltpu.VMEM((2 * tokens, HEAD_WIDTH), BF16),
            pltpu.VMEM((2 * tokens // BLOCK, BLOCK), jnp.int32),
        ],
        compiler_params=pltpu.CompilerParams(vmem_limit_bytes=40 * 1024 * 1024),
        name="attend",
    )(q, lowrank, up, kpage, vpage, kprev, vprev, k, v, code, ids, idprev)


def solution(mesh, nz=8):
    groups, ntp = mesh.shape["grp"], mesh.shape["tp"]
    ny = groups // nz

    def local(x, q, k, v, request, cache, down, up, page_list, adapter_list, page_entry, adapter_entry):
        listed = adapter_list.shape[1]
        ids = request.reshape(-1, BLOCK)
        entries = (page_entry * listed + adapter_entry).reshape(1, -1)
        lowrank, up_own, kpage, vpage, kprev, vprev, code, idprev = fetch(
            ny, nz, ntp, page_list, adapter_list, ids, entries, x, k, v, cache, down, up
        )
        return attend(q, lowrank, up_own, kpage, vpage, kprev, vprev, k, v, code, ids, idprev)

    placed = (
        P("grp", "tp"),
        P("grp", "tp"),
        P("grp", "tp"),
        P("grp", "tp"),
        P("grp"),
        P("grp", None, None, "tp"),
        P("grp", None, "tp"),
        P("grp", None, "tp"),
        P(),
        P(),
        P(),
        P(),
    )
    return jax.shard_map(local, mesh=mesh, in_specs=placed, out_specs=P("grp", "tp"), check_vma=False)
```

time: 373 us -> 96.3 us (0.26)
  the two profiles are of different devices: /device:TPU:6 before, /device:TPU:1 now
where the time goes in v1:
time: 96.3 us; the launch traced here: 95.9 us
  Pallas kernels  89.7 us (93%)
  local copies, waits for them, and re-layouts  5.51 us (6%)
    pallas_call x1, Pallas kernels, fetch(): pl.pallas_call(functools.partial(fetch_kernel, ny, nz, ntp), out_shape=(s...  70.6 us
    pallas_call x1, Pallas kernels, attend(): pl.pallas_call(attend_kernel, grid=(tokens // BLOCK,), out_shape=jax.Shap...  19.1 us
    unnamed x28, local copies, waits for them, and re-layouts  5.51 us

profile of v1, /device:TPU:1, one launch (start us, length us, event | category | flops | bytes accessed | tf_op | source)
XLA Modules:
  0.0 95.9 jit_solution(1640106846408243620)
XLA Ops:
  0.0 0.0 copy-start.12
  0.0 0.7 copy-done.12
  0.7 0.0 copy-start.10
  0.7 0.0 copy-start.11
  0.7 0.7 multiply_add_fusion
  1.4 0.0 copy-done.10
  1.4 0.0 copy-start.7
  1.4 0.0 copy-start.8
  1.4 0.1 copy.13.page_list
  1.5 0.0 copy-done.11
  1.5 0.0 copy-start.9
  1.5 0.1 copy.14.adapter_list
  1.6 0.5 copy-done.7
  2.2 0.0 copy-done.8
  2.2 0.0 copy-done.9
  2.2 1.2 %copy-done = bf16[1024,512]{1,0:T(8,128)(2,1)S(1)} copy-done((bf16[1024,512]{1,0:T(8,128)(2,1)S(1)}, bf16[1024,512]{1,0:T(8,128)(2,1)}, u32[]{:S(2)}) %copy-start) | copy-done | bytes 1048600
  3.4 0.9 copy-done.2
  4.4 0.9 copy-done.4
  5.3 0.9 copy-done.6
  6.2 70.6 %fetch.1 = (bf16[8,16,128]{2,1,0:T(8,128)(2,1)S(1)}, bf16[4,16,512]{2,1,0:T(8,128)(2,1)S(1)}, bf16[512,128]{1,0:T(8,128)(2,1)S(1)}, bf16[512,128]{1,0:T(8,128)(2...) custom-call(s32[64,4]{1,0:T(8,128)S(1)} %copy.13.page_list, ...), custom_call_target="tpu_custom_call" | custom-call | tf_op jit(solution)/shard_map/fetch/pallas_call | solution.py:381
  76.8 0.0 copy-done.1
  76.9 0.0 copy-done.3
  76.9 0.0 copy-done.5
  76.9 19.1 %attend.1 = bf16[1024,512]{1,0:T(8,128)(2,1)} custom-call(bf16[1024,512]{1,0:T(8,128)(2,1)S(1)} %copy-done.1, bf16[8,16,128]{2,1,0:T(8,128)(2,1)S(1)} %get-tuple-element.13.lowrank_ref, bf16[4,16,512]{2,1,0:T(8,128)(2,1)S(1)} %get-tuple-element.14.up_ref, bf16[512,128]{1,0:T(8,128)(2,1)S(1)} %get-tuple-element.15.kpage_ref, ...), custom_call_target="tpu_custom_call" | custom-call | tf_op jit(solution)/shard_map/attend/pallas_call | solution.py:422
  (7 shorter events, 0.0 us)
Async XLA Ops:
  0.0 0.7 copy-start.12
  0.7 0.7 copy-start.10
  0.7 0.8 copy-start.11
  1.4 0.8 copy-start.7
  1.4 0.8 copy-start.8
  1.5 0.7 copy-start.9
  2.2 1.2 %copy-start = (bf16[1024,512]{1,0:T(8,128)(2,1)S(1)}, bf16[1024,512]{1,0:T(8,128)(2,1)}, u32[]{:S(2)}) copy-start(bf16[1024,512]{1,0:T(8,128)(2,1)} %x_ref.1) | copy-start | bytes 3145732
  3.4 0.9 copy-start.2
  4.4 0.9 copy-start.4
  5.3 0.9 copy-start.6
  6.2 70.6 %copy-start.1 = (bf16[1024,512]{1,0:T(8,128)(2,1)S(1)}, bf16[1024,512]{1,0:T(8,128)(2,1)}, u32[]{:S(2)}) copy-start(bf16[1024,512]{1,0:T(8,128)(2,1)} %q_ref.1) | copy-start | bytes 3145732
  6.2 70.6 %copy-start.3 = (bf16[1024,128]{1,0:T(8,128)(2,1)S(1)}, bf16[1024,128]{1,0:T(8,128)(2,1)}, u32[]{:S(2)}) copy-start(bf16[1024,128]{1,0:T(8,128)(2,1)} %k_ref.3) | copy-start | bytes 786436
  6.2 70.6 %copy-start.5 = (bf16[1024,128]{1,0:T(8,128)(2,1)S(1)}, bf16[1024,128]{1,0:T(8,128)(2,1)}, u32[]{:S(2)}) copy-start(bf16[1024,128]{1,0:T(8,128)(2,1)} %v_ref.3) | copy-start | bytes 786436

commit v2 on v1

v2 whole, which is shorter than its diff:
```python
import functools
import math

import jax
import jax.numpy as jnp
from jax import lax
from jax.experimental import pallas as pl
from jax.experimental.pallas import tpu as pltpu
from jax.sharding import PartitionSpec as P

PER_KV = 4
HEAD_WIDTH = 128
PAGE = 128
BLOCK = 128
ADAPTER_SCALE = 0.5
MESH = pl.DeviceIdType.MESH
F32 = jnp.float32
BF16 = jnp.bfloat16


def ring_split(n, heavy_right):
    more, fewer = n // 2, (n - 1) // 2
    return (more, fewer) if heavy_right else (fewer, more)


def token_codes(ids_row, table_columns):
    requests = table_columns.shape[0]
    numbers = lax.broadcasted_iota(jnp.int32, (requests, ids_row.shape[1]), 0)
    return jnp.sum(jnp.where(numbers == ids_row, table_columns, 0), axis=0, keepdims=True)


def as_columns(row):
    return jnp.broadcast_to(row, (128, row.shape[1])).T


class Gather:
    def __init__(self, table, pos, n, peers, split, send, recv):
        self.copies = []
        for s in range(1, max(split) + 1):
            now = []
            for way in (0, 1):
                if s <= split[way]:
                    origin = lax.rem(pos - (s - 1) + n, n) if way == 0 else lax.rem(pos + (s - 1), n)
                    at = s - 1 if way == 0 else split[0] + s - 1
                    now.append(remote(table.at[origin], table.at[origin], send.at[at], recv.at[at], peers[way]))
                else:
                    now.append(None)
            self.copies.append(now)
        self.steps = len(self.copies)

    def start(self):
        for copy in self.copies[0]:
            if copy is not None:
                copy.start()

    def forward(self, s):
        for way, copy in enumerate(self.copies[s]):
            if copy is not None:
                copy.wait_recv()
                if s + 1 < self.steps and self.copies[s + 1][way] is not None:
                    self.copies[s + 1][way].start()

    def finish(self):
        for now in self.copies:
            for copy in now:
                if copy is not None:
                    copy.wait_send()


class Slots:
    def __init__(self, load, lists, picks, slots, pos, n, peers, split, send, recv, group_at, index_of, place_of):
        self.load, self.lists, self.picks, self.slots, self.pos, self.n = load, lists, picks, slots, pos, n
        self.split = split
        self.base = (0, split[0] + 1)
        self.group_at, self.index_of, self.place_of = group_at, index_of, place_of
        self.copies = []
        for way in (0, 1):
            base = self.base[way]
            sems = 0 if way == 0 else split[0]
            self.copies.append(
                [
                    remote(slots.at[base + s], slots.at[base + s + 1], send.at[sems + s], recv.at[sems + s], peers[way])
                    for s in range(split[way])
                ]
            )
        self.steps = max(split)
        self.plan = {}

    def prepare(self):
        for way in (0, 1):
            for s in range(self.split[way] + 1):
                away = self.split[way] - s
                target = lax.rem(self.pos + away, self.n) if way == 0 else lax.rem(self.pos - away + self.n, self.n)
                group = self.group_at(target)
                items = [self.lists[k, group] for k in self.picks]
                self.plan[way, s] = [(self.index_of(item), self.place_of(item)) for item in items]

    def fill(self, way, s, wait=None):
        plan = self.plan[way, s]
        mine = [self.load(index) for index, _ in plan]
        if wait is not None:
            wait()
        at = self.base[way] + s
        for k, (_, place) in enumerate(plan):
            value = mine[k]
            if s > 0:
                value = jnp.where(place == self.pos, value, self.slots[at, k])
            self.slots[at, k] = value

    def start(self):
        for way in (0, 1):
            if self.split[way] > 0:
                self.fill(way, 0)
                self.copies[way][0].start()

    def forward(self, s):
        for way in (0, 1):
            if s < self.split[way]:
                copy = self.copies[way][s]
                if s + 1 < self.split[way]:
                    self.fill(way, s + 1, copy.wait_recv)
                    self.copies[way][s + 1].start()
                else:
                    copy.wait_recv()

    def entry(self, k):
        rights, lefts = self.split
        index, place = self.plan[0, rights][k]
        value = self.load(index)
        ahead = lax.rem(place - self.pos + self.n, self.n)
        if rights > 0:
            value = jnp.where(ahead > lefts, self.slots[rights, k], value)
        if lefts > 0:
            value = jnp.where((ahead > 0) & (ahead <= lefts), self.slots[rights + 1 + lefts, k], value)
        return value

    def finish(self):
        for way in (0, 1):
            for copy in self.copies[way]:
                copy.wait_send()


def remote(src, dst, send, recv, peer):
    return pltpu.make_async_remote_copy(
        src_ref=src, dst_ref=dst, send_sem=send, recv_sem=recv, device_id=peer, device_id_type=MESH
    )


PREV_PARTS = 4
FACTOR = math.log2(math.e) * HEAD_WIDTH ** -0.5
NT = (((1,), (1,)), ((), ()))
TN = (((0,), (0,)), ((), ()))


def fused_kernel(
    ny, nz, ntp,
    page_list, adapter_list, page_entry_ref, adapter_entry_ref,
    ids_hbm, x_hbm, q_hbm, k_hbm, v_hbm, cache_hbm, down_hbm, up_hbm,
    out_hbm,
    down_tab, up_tab, kpage_tab, vpage_tab,
    down_slots, up_slots, kpage_slots, vpage_slots,
    x_ref, q_ref, ids_ref, idprev_ref, code_ref, down_all, up_all,
    keys, values, values_t, key_ids, kpages, vpages_t,
    parts, from_pair, half_sum, from_x, lowrank_ref,
    queries, tops, sums_ref, mixed_ref, out_ref,
    gather_send, gather_recv, slot_send, slot_recv, prev_send, prev_recv, pair_send, pair_recv, x_send, x_recv,
    here, done,
):
    group = lax.axis_index("grp")
    tp = lax.axis_index("tp")
    groups = ny * nz
    y, z = lax.div(group, nz), lax.rem(group, nz)
    z_peers = ((y * nz + lax.rem(z + 1, nz), tp), (y * nz + lax.rem(z + nz - 1, nz), tp))
    y_peers = ((lax.rem(y + 1, ny) * nz + z, tp), (lax.rem(y + ny - 1, ny) * nz + z, tp))
    after = (lax.rem(group + 1, groups), tp)
    before = (lax.rem(group + groups - 1, groups), tp)
    core = lax.rem(tp, 2)
    pair = (group, tp + 1 - 2 * core)
    x_peers = [(group, lax.rem(tp + 2 * d, ntp)) for d in range(1, ntp // 2)]

    barrier = pltpu.get_barrier_semaphore()
    greeted = [z_peers[0], z_peers[1], y_peers[0], y_peers[1], after, before, pair] + x_peers
    for peer in greeted:
        pl.semaphore_signal(barrier, inc=1, device_id=peer, device_id_type=MESH)

    stored, rank = down_hbm.shape[0], down_hbm.shape[1]
    tokens = k_hbm.shape[0]
    chunks = tokens // BLOCK
    listed, plisted = adapter_list.shape[0], page_list.shape[0]
    half = plisted // 2

    own = [
        pltpu.make_async_copy(down_hbm, down_tab.at[z], here.at[0]),
        pltpu.make_async_copy(up_hbm, up_tab.at[y], here.at[1]),
        pltpu.make_async_copy(cache_hbm.at[:, 0], kpage_tab.at[z], here.at[2]),
        pltpu.make_async_copy(cache_hbm.at[:, 1], vpage_tab.at[y], here.at[3]),
    ]
    own_rows = pl.ds(tokens, tokens)
    staged = [
        pltpu.make_async_copy(ids_hbm, ids_ref, here.at[4]),
        pltpu.make_async_copy(x_hbm, x_ref, here.at[5]),
        pltpu.make_async_copy(q_hbm, q_ref, here.at[6]),
        pltpu.make_async_copy(k_hbm, keys.at[own_rows], here.at[7]),
        pltpu.make_async_copy(v_hbm, values.at[own_rows], here.at[8]),
    ]
    for copy in own + staged:
        copy.start()

    zs, ys = ring_split(nz, False), ring_split(ny, True)
    gathers = [
        Gather(down_tab, z, nz, z_peers, zs, gather_send.at[0], gather_recv.at[0]),
        Gather(up_tab, y, ny, y_peers, ys, gather_send.at[1], gather_recv.at[1]),
        Gather(kpage_tab, z, nz, z_peers, zs, gather_send.at[2], gather_recv.at[2]),
        Gather(vpage_tab, y, ny, y_peers, ys, gather_send.at[3], gather_recv.at[3]),
    ]

    def along_y(table, lists, picks, slots, at):
        return Slots(
            lambda index: table[index], lists, picks, slots, y, ny, y_peers, ys, slot_send.at[at], slot_recv.at[at],
            lambda target: target * nz + z,
            lambda item: (lax.rem(lax.div(item, stored), nz), lax.rem(item, stored)),
            lambda item: lax.div(item, stored * nz),
        )

    def along_z(table, lists, picks, slots, at):
        return Slots(
            lambda index: table[index], lists, picks, slots, z, nz, z_peers, zs, slot_send.at[at], slot_recv.at[at],
            lambda target: y * nz + target,
            lambda item: (lax.div(item, stored * nz), lax.rem(item, stored)),
            lambda item: lax.rem(lax.div(item, stored), nz),
        )

    downs = along_y(down_tab, adapter_list, range(listed), down_slots, 0)
    ups = along_z(up_tab, adapter_list, range(listed), up_slots, 1)
    pages = [
        ring
        for part in range(2)
        for ring in (
            along_y(kpage_tab, page_list, range(part * half, part * half + half), kpage_slots.at[part], 2 + part),
            along_z(vpage_tab, page_list, range(part * half, part * half + half), vpage_slots.at[part], 4 + part),
        )
    ]

    rows = tokens // PREV_PARTS
    prevs = []
    for part in range(PREV_PARTS):
        at = pl.ds(part * rows, rows)
        prevs.append(remote(k_hbm.at[at], keys.at[at], prev_send.at[0, part], prev_recv.at[0, part], after))
        prevs.append(remote(v_hbm.at[at], values.at[at], prev_send.at[1, part], prev_recv.at[1, part], after))
    idprev = remote(ids_hbm, idprev_ref, prev_send.at[2, 0], prev_recv.at[2, 0], after)
    waiting = list(prevs)

    def some_prev(count):
        for _ in range(min(count, len(waiting))):
            waiting.pop(0).start()

    pl.semaphore_wait(barrier, len(greeted))
    for copy, gather in zip(own, gathers):
        copy.wait()
        gather.start()
    idprev.start()
    some_prev(1)

    for ring in [downs, ups] + pages:
        ring.prepare()
    staged[0].wait()
    code_columns = as_columns(page_entry_ref[...] * listed + adapter_entry_ref[...])
    for c in range(chunks):
        code_ref[pl.ds(c, 1), :] = token_codes(ids_ref[pl.ds(c, 1), :], code_columns)
        key_ids[pl.ds(tokens + c * BLOCK, BLOCK), :] = as_columns(ids_ref[pl.ds(c, 1), :])

    gsteps = max(g.steps for g in gathers)

    def gather_step(which, s):
        for gather in which:
            if 0 <= s < gather.steps:
                gather.forward(s)

    def slot_step(which, s):
        for ring in which:
            if 0 <= s < ring.steps:
                ring.forward(s)

    for s in range(gsteps):
        gather_step(gathers[:2], s)
        gather_step(gathers[2:], s - 1)
        some_prev(1)
    downs.start()
    ups.start()
    gather_step(gathers[2:], gsteps - 1)
    slot_step([downs], 0)
    for ring in pages:
        ring.start()
    slot_step([ups], 0)
    steps = max(downs.steps, ups.steps)
    for s in range(1, steps):
        slot_step([downs], s)
        slot_step([ups], s)
        if s + 1 < steps:
            slot_step(pages, s - 1)
        some_prev(2)
    some_prev(len(waiting))
    served = max(steps - 2, 0)

    for k in range(listed):
        down_all[k * rank:(k + 1) * rank, :] = downs.entry(k)
    staged[1].wait()
    partial = lax.dot_general(down_all[...], x_ref[...], NT, preferred_element_type=F32)
    for c in range(chunks):
        entry = lax.rem(code_ref[pl.ds(c, 1), :], listed)
        total = jnp.zeros((rank, BLOCK), F32)
        for k in range(listed):
            total = jnp.where(entry == k, partial[k * rank:(k + 1) * rank, c * BLOCK:(c + 1) * BLOCK], total)
        parts[c] = total
    each = chunks // 2
    mine = pl.ds(core * each, each)
    theirs = pl.ds((1 - core) * each, each)
    to_pair = remote(parts.at[theirs], from_pair, pair_send.at[0], pair_recv.at[0], pair)
    to_pair.start()
    to_pair.wait_recv()
    half_sum[...] = parts[mine] + from_pair[...]
    to_x = [
        remote(half_sum, from_x.at[d], x_send.at[d], x_recv.at[d], peer) for d, peer in enumerate(x_peers)
    ]
    for copy in to_x:
        copy.start()

    for k in range(listed):
        up_all[k * rank:(k + 1) * rank, :] = ups.entry(k)
    for copy in staged[2:]:
        copy.wait()
    for c in range(chunks):
        at = tokens + c * BLOCK
        values_t[:, at:at + BLOCK] = values[at:at + BLOCK, :].T
    if served + 1 < steps:
        slot_step(pages, served)
        served += 1
    for copy in prevs + [idprev]:
        copy.wait_recv()
    first = group == 0
    for c in range(chunks):
        at = c * BLOCK
        values_t[:, at:at + BLOCK] = values[at:at + BLOCK, :].T
        key_ids[at:at + BLOCK, :] = as_columns(jnp.where(first, -1, idprev_ref[pl.ds(c, 1), :]))

    total = half_sum[...]
    for d, copy in enumerate(to_x):
        copy.wait_recv()
        total = total + from_x[d]
    lowrank_ref[mine] = total.astype(BF16)
    back = remote(lowrank_ref.at[mine], lowrank_ref.at[mine], pair_send.at[1], pair_recv.at[1], pair)
    back.start()
    back.wait_recv()

    band = tokens + BLOCK
    later = lax.broadcasted_iota(jnp.int32, (BLOCK, BLOCK), 0)
    sooner = lax.broadcasted_iota(jnp.int32, (BLOCK, BLOCK), 1)
    causal = later <= sooner

    def band_block(i, carry):
        start = pl.multiple_of(i * BLOCK, BLOCK)
        entry = lax.rem(code_ref[pl.ds(i, 1), :], listed)
        low = lowrank_ref[i]
        wide = jnp.concatenate([jnp.where(entry == k, low, jnp.zeros_like(low)) for k in range(listed)], axis=0)
        update = lax.dot_general(wide, up_all[...], TN, preferred_element_type=F32)
        query = (q_ref[pl.ds(start, BLOCK), :].astype(F32) + ADAPTER_SCALE * update).astype(BF16)
        stacked = jnp.concatenate([query[:, h * HEAD_WIDTH:(h + 1) * HEAD_WIDTH] for h in range(PER_KV)], axis=0)
        queries[i] = stacked
        scores = lax.dot_general(keys[pl.ds(start, band), :], stacked, NT, preferred_element_type=F32)
        ids_row = ids_ref[pl.ds(i, 1), :]
        masks = [key_ids[pl.ds(start + c * BLOCK, BLOCK), :] == ids_row for c in range(chunks + 1)]
        masks[chunks] = masks[chunks] & causal
        weights = []
        for h in range(PER_KV):
            across = slice(h * BLOCK, (h + 1) * BLOCK)
            pieces = [
                jnp.where(masks[c], scores[c * BLOCK:(c + 1) * BLOCK, across], F32(-1e30)) for c in range(chunks + 1)
            ]
            top = jnp.max(functools.reduce(jnp.maximum, pieces), axis=0, keepdims=True)
            expos = [jnp.exp2((piece - top) * FACTOR) for piece in pieces]
            tops[i, h:h + 1, :] = top
            sums_ref[i, h:h + 1, :] = jnp.sum(functools.reduce(jnp.add, expos), axis=0, keepdims=True)
            weights.append(jnp.concatenate([e.astype(BF16) for e in expos], axis=0))
        mixed_ref[i] = jnp.dot(
            values_t[:, pl.ds(start, band)], jnp.concatenate(weights, axis=1), preferred_element_type=F32
        )
        return carry

    while served + 1 < steps:
        slot_step(pages, served)
        served += 1
    lax.fori_loop(0, chunks, band_block, 0, unroll=2)
    slot_step(pages, served)

    for part in range(2):
        for k in range(half):
            at = (part * half + k) * PAGE
            kpages[at:at + PAGE, :] = pages[2 * part].entry(k)
            vpages_t[:, at:at + PAGE] = pages[2 * part + 1].entry(k).T

    def page_block(i, carry):
        start = pl.multiple_of(i * BLOCK, BLOCK)
        scores = lax.dot_general(kpages[...], queries[i], NT, preferred_element_type=F32)
        page_of = lax.div(code_ref[pl.ds(i, 1), :], listed)
        weights, scales = [], []
        for h in range(PER_KV):
            across = slice(h * BLOCK, (h + 1) * BLOCK)
            piece = scores[:PAGE, across]
            for k in range(1, plisted):
                piece = jnp.where(page_of == k, scores[k * PAGE:(k + 1) * PAGE, across], piece)
            before_top = tops[i, h:h + 1, :]
            top = jnp.maximum(jnp.max(piece, axis=0, keepdims=True), before_top)
            expo = jnp.exp2((piece - top) * FACTOR)
            shrink = jnp.exp2((before_top - top) * FACTOR)
            total = sums_ref[i, h:h + 1, :] * shrink + jnp.sum(expo, axis=0, keepdims=True)
            scales.append((shrink, 1.0 / total))
            weights.append(
                jnp.concatenate([jnp.where(page_of == k, expo, 0.0).astype(BF16) for k in range(plisted)], axis=0)
            )
        mixed = jnp.dot(vpages_t[...], jnp.concatenate(weights, axis=1), preferred_element_type=F32)
        for h in range(PER_KV):
            across = slice(h * BLOCK, (h + 1) * BLOCK)
            shrink, inverse = scales[h]
            value = (mixed_ref[i, :, across] * shrink + mixed[:, across]) * inverse
            out_ref[pl.ds(start, BLOCK), h * HEAD_WIDTH:(h + 1) * HEAD_WIDTH] = value.T.astype(BF16)
        at = pl.ds(start, BLOCK)
        pltpu.make_async_copy(out_ref.at[at], out_hbm.at[at], done.at[i]).start()
        return carry

    lax.fori_loop(0, chunks, page_block, 0, unroll=2)

    for copy in prevs + [idprev, to_pair, back] + to_x:
        copy.wait_send()
    for ring in gathers + [downs, ups] + pages:
        ring.finish()
    for i in range(chunks):
        at = pl.ds(i * BLOCK, BLOCK)
        pltpu.make_async_copy(out_ref.at[at], out_hbm.at[at], done.at[i]).wait()


def fused(ny, nz, ntp, page_list, adapter_list, page_entry, adapter_entry, ids, x, q, k, v, cache, down, up):
    chunks = ids.shape[0]
    tokens = k.shape[0]
    stored, rank, features = down.shape
    listed, plisted = adapter_list.shape[0], page_list.shape[0]
    half = plisted // 2
    vmem = pl.BlockSpec(memory_space=pltpu.VMEM)
    smem = pl.BlockSpec(memory_space=pltpu.SMEM)
    hbm = pl.BlockSpec(memory_space=pltpu.HBM)
    most = max(ny, nz) - 1
    nx = max(ntp // 2 - 1, 1)
    dma = pltpu.SemaphoreType.DMA
    stack = PER_KV * BLOCK
    return pl.pallas_call(
        functools.partial(fused_kernel, ny, nz, ntp),
        out_shape=jax.ShapeDtypeStruct(q.shape, BF16),
        in_specs=[smem, smem, vmem, vmem] + [hbm] * 8,
        out_specs=hbm,
        scratch_shapes=[
            pltpu.VMEM((nz, stored, rank, features), BF16),
            pltpu.VMEM((ny, stored, rank, features), BF16),
            pltpu.VMEM((nz, stored, PAGE, HEAD_WIDTH), BF16),
            pltpu.VMEM((ny, stored, PAGE, HEAD_WIDTH), BF16),
            pltpu.VMEM((ny + 1, listed, rank, features), BF16),
            pltpu.VMEM((nz + 1, listed, rank, features), BF16),
            pltpu.VMEM((2, ny + 1, half, PAGE, HEAD_WIDTH), BF16),
            pltpu.VMEM((2, nz + 1, half, PAGE, HEAD_WIDTH), BF16),
            pltpu.VMEM(x.shape, BF16),
            pltpu.VMEM(q.shape, BF16),
            pltpu.VMEM(ids.shape, jnp.int32),
            pltpu.VMEM(ids.shape, jnp.int32),
            pltpu.VMEM(ids.shape, jnp.int32),
            pltpu.VMEM((listed * rank, features), BF16),
            pltpu.VMEM((listed * rank, features), BF16),
            pltpu.VMEM((2 * tokens, HEAD_WIDTH), BF16),
            pltpu.VMEM((2 * tokens, HEAD_WIDTH), BF16),
            pltpu.VMEM((HEAD_WIDTH, 2 * tokens), BF16),
            pltpu.VMEM((2 * tokens, BLOCK), jnp.int32),
            pltpu.VMEM((plisted * PAGE, HEAD_WIDTH), BF16),
            pltpu.VMEM((HEAD_WIDTH, plisted * PAGE), BF16),
            pltpu.VMEM((chunks, rank, BLOCK), F32),
            pltpu.VMEM((chunks // 2, rank, BLOCK), F32),
            pltpu.VMEM((chunks // 2, rank, BLOCK), F32),
            pltpu.VMEM((nx, chunks // 2, rank, BLOCK), F32),
            pltpu.VMEM((chunks, rank, BLOCK), BF16),
            pltpu.VMEM((chunks, stack, HEAD_WIDTH), BF16),
            pltpu.VMEM((chunks, 8, BLOCK), F32),
            pltpu.VMEM((chunks, 8, BLOCK), F32),
            pltpu.VMEM((chunks, HEAD_WIDTH, stack), F32),
            pltpu.VMEM(q.shape, BF16),
            dma((4, most)), dma((4, most)), dma((6, most)), dma((6, most)),
            dma((3, PREV_PARTS)), dma((3, PREV_PARTS)),
            dma((2,)), dma((2,)), dma((nx,)), dma((nx,)),
            dma((9,)), dma((chunks,)),
        ],
        compiler_params=pltpu.CompilerParams(
            collective_id=0, has_side_effects=True, vmem_limit_bytes=56 * 1024 * 1024
        ),
        name="fused",
    )(page_list, adapter_list, page_entry, adapter_entry, ids, x, q, k, v, cache, down, up)


def solution(mesh, nz=8):
    groups, ntp = mesh.shape["grp"], mesh.shape["tp"]
    ny = groups // nz

    def local(x, q, k, v, request, cache, down, up, page_list, adapter_list, page_entry, adapter_entry):
        return fused(
            ny, nz, ntp, page_list.T, adapter_list.T, page_entry.reshape(1, -1), adapter_entry.reshape(1, -1),
            request.reshape(-1, BLOCK), x, q, k, v, cache, down, up,
        )

    placed = (
        P("grp", "tp"),
        P("grp", "tp"),
        P("grp", "tp"),
        P("grp", "tp"),
        P("grp"),
        P("grp", None, None, "tp"),
        P("grp", None, "tp"),
        P("grp", None, "tp"),
        P(),
        P(),
        P(),
        P(),
    )
    return jax.shard_map(local, mesh=mesh, in_specs=placed, out_specs=P("grp", "tp"), check_vma=False)
```

time: 96.3 us -> 78 us (0.81)
  Pallas kernels: 89.7 us -> 75.5 us
  local copies, waits for them, and re-layouts: 5.51 us -> 2.26 us
    pallas_call x2 -> x1, Pallas kernels: 89.7 us -> 75.5 us  [fused(): pl.pallas_call(functools.partial(fused_kernel, ny, nz, ntp), out_shape=ja...]
    unnamed x28 -> x1, local copies, waits for them, and re-layouts: 5.51 us -> 2.26 us
where the time goes in v2:
time: 78 us; the launch traced here: 77.8 us
  Pallas kernels  75.5 us (97%)
  local copies, waits for them, and re-layouts  2.26 us (3%)
    pallas_call x1, Pallas kernels, fused(): pl.pallas_call(functools.partial(fused_kernel, ny, nz, ntp), out_shape=ja...  75.5 us
    unnamed x1, local copies, waits for them, and re-layouts  2.26 us

profile of v2, /device:TPU:1, one launch (start us, length us, event | category | flops | bytes accessed | tf_op | source)
XLA Modules:
  0.0 77.8 jit_solution(4332904200464412953)
XLA Ops:
  0.0 75.5 %fused.1 = bf16[1024,512]{1,0:T(8,128)(2,1)} custom-call(s32[4,64]{1,0:T(4,128)} %bitcast.6, s32[4,64]{1,0:T(4,128)} %bitcast.7, s32[1,256]{1,0:T(1,128)} %bitcast.8, s32[1,256]{1,0:T(1,128)} %bitcast.9, s32[8,128]{1,0:T(8,128)} %bitcast.5, bf16[1024,512]{1,0:T(8,128)(2,1)} %x_hbm.1, bf16[1024,512]{1,0:T(8,128)(2,1)} %q_hbm.1, bf16[1024,128]{1,0:T(8,128)(2,1)} %k_hbm.1, ...), custom_call_target="tpu_custom_call" | custom-call | tf_op jit(solution)/shard_map/fused/pallas_call | solution.py:454
  75.5 2.3 %copy.14 = bf16[1024,512]{1,0:T(8,128)(2,1)} copy(bf16[1024,512]{1,0:T(8,128)(2,1)} %fused.1) | data formatting | bytes 2097152

commit v3 on v2

--- a/solution.py
+++ b/solution.py
@@ -140,6 +140,91 @@
                 copy.wait_send()
 
 
+class Spread:
+    def __init__(self, table, pos, n, peer_at, send, recv):
+        order = sorted(range(1, n), key=lambda d: -min(d, n - d))
+        self.copies = [remote(table.at[pos], table.at[pos], send.at[d - 1], recv.at[d - 1], peer_at(d)) for d in order]
+
+    def start(self):
+        for copy in self.copies:
+            copy.start()
+
+    steps = 1
+
+    def forward(self, s):
+        for copy in self.copies:
+            copy.wait_recv()
+
+    def finish(self):
+        for copy in self.copies:
+            copy.wait_send()
+
+
+CHAINS = {8: ((-4, -3), (-2, -1), (2, 1), (3,)), 4: ((-2, -1), (1,)), 2: ((-1,),)}
+
+
+class Relay:
+    def __init__(self, table, lists, slots, pos, n, peer_at, send, recv, group_at, index_of, place_of):
+        self.table, self.slots, self.pos, self.n = table, slots, pos, n
+        self.chains = CHAINS[n]
+        self.plan, self.first, self.second = {}, [], []
+        count = lists.shape[0]
+        targets = [0] + [-offset for chain in self.chains for offset in chain]
+        for away in targets:
+            group = group_at(lax.rem(pos + away + n, n))
+            items = [lists[k, group] for k in range(count)]
+            self.plan[away] = [(index_of(item), place_of(item)) for item in items]
+        for c, chain in enumerate(self.chains):
+            at = 3 * c
+            if len(chain) == 1:
+                self.first.append(remote(slots.at[at], slots.at[at + 2], send.at[c, 0], recv.at[c, 0], peer_at(-chain[0])))
+                self.second.append(None)
+            else:
+                self.first.append(
+                    remote(slots.at[at], slots.at[at + 1], send.at[c, 0], recv.at[c, 0], peer_at(chain[1] - chain[0]))
+                )
+                self.second.append(
+                    remote(slots.at[at + 1], slots.at[at + 2], send.at[c, 1], recv.at[c, 1], peer_at(-chain[1]))
+                )
+
+    def start(self):
+        for c, chain in enumerate(self.chains):
+            for k, (index, _) in enumerate(self.plan[-chain[0]]):
+                self.slots[3 * c, k] = self.table[index]
+            self.first[c].start()
+
+    steps = 2
+
+    def forward(self, s):
+        if s == 1:
+            for c, chain in enumerate(self.chains):
+                (self.first if len(chain) == 1 else self.second)[c].wait_recv()
+            return
+        for c, chain in enumerate(self.chains):
+            if len(chain) == 2:
+                plan = self.plan[-chain[1]]
+                mine = [self.table[index] for index, _ in plan]
+                self.first[c].wait_recv()
+                for k, (_, place) in enumerate(plan):
+                    self.slots[3 * c + 1, k] = jnp.where(place == self.pos, mine[k], self.slots[3 * c + 1, k])
+                self.second[c].start()
+
+    def entry(self, k):
+        index, place = self.plan[0][k]
+        value = self.table[index]
+        ahead = lax.rem(place - self.pos + self.n, self.n)
+        for c, chain in enumerate(self.chains):
+            here = ahead == (chain[0] + self.n) % self.n
+            if len(chain) == 2:
+                here = here | (ahead == (chain[1] + self.n) % self.n)
+            value = jnp.where(here, self.slots[3 * c + 2, k], value)
+        return value
+
+    def finish(self):
+        for copy in self.first + [copy for copy in self.second if copy is not None]:
+            copy.wait_send()
+
+
 def remote(src, dst, send, recv, peer):
     return pltpu.make_async_remote_copy(
         src_ref=src, dst_ref=dst, send_sem=send, recv_sem=recv, device_id=peer, device_id_type=MESH
@@ -147,6 +232,13 @@
 
 
 PREV_PARTS = 4
+DIRECT = "du"
+SCHEDULE = (
+    "D0", "U0", "K0", "V0", "p1", "D1", "U1", "K1", "V1", "p1", "D2", "U2",
+    "K2", "V2", "p2", "D3", "U3", "d*", "u*", "K3", "V3", "d0", "u0", "p8",
+    "k*", "v*", "P", "O", "k0", "v0", "R", "k1", "v1", "B", "B", "k2",
+    "v2", "B", "B",
+)
 FACTOR = math.log2(math.e) * HEAD_WIDTH ** -0.5
 NT = (((1,), (1,)), ((), ()))
 TN = (((0,), (0,)), ((), ()))
@@ -163,7 +255,7 @@
     keys, values, values_t, key_ids, kpages, vpages_t,
     parts, from_pair, half_sum, from_x, lowrank_ref,
     queries, tops, sums_ref, mixed_ref, out_ref,
-    gather_send, gather_recv, slot_send, slot_recv, prev_send, prev_recv, pair_send, pair_recv, x_send, x_recv,
+    gather_send, gather_recv, relay_send, relay_recv, slot_send, slot_recv, prev_send, prev_recv, pair_send, pair_recv, x_send, x_recv,
     here, done,
 ):
     group = lax.axis_index("grp")
@@ -179,7 +271,13 @@
     x_peers = [(group, lax.rem(tp + 2 * d, ntp)) for d in range(1, ntp // 2)]
 
     barrier = pltpu.get_barrier_semaphore()
-    greeted = [z_peers[0], z_peers[1], y_peers[0], y_peers[1], after, before, pair] + x_peers
+    def z_at(offset):
+        return (y * nz + lax.rem(z + offset + nz, nz), tp)
+
+    def y_at(offset):
+        return (lax.rem(y + offset + ny, ny) * nz + z, tp)
+
+    greeted = [z_at(d) for d in range(1, nz)] + [y_at(d) for d in range(1, ny)] + [after, before, pair] + x_peers
     for peer in greeted:
         pl.semaphore_signal(barrier, inc=1, device_id=peer, device_id_type=MESH)
 
@@ -207,39 +305,65 @@
         copy.start()
 
     zs, ys = ring_split(nz, False), ring_split(ny, True)
-    gathers = [
-        Gather(down_tab, z, nz, z_peers, zs, gather_send.at[0], gather_recv.at[0]),
-        Gather(up_tab, y, ny, y_peers, ys, gather_send.at[1], gather_recv.at[1]),
-        Gather(kpage_tab, z, nz, z_peers, zs, gather_send.at[2], gather_recv.at[2]),
-        Gather(vpage_tab, y, ny, y_peers, ys, gather_send.at[3], gather_recv.at[3]),
-    ]
-
-    def along_y(table, lists, picks, slots, at):
-        return Slots(
-            lambda index: table[index], lists, picks, slots, y, ny, y_peers, ys, slot_send.at[at], slot_recv.at[at],
-            lambda target: target * nz + z,
-            lambda item: (lax.rem(lax.div(item, stored), nz), lax.rem(item, stored)),
-            lambda item: lax.div(item, stored * nz),
+    by_y = (lambda target: target * nz + z, lambda item: (lax.rem(lax.div(item, stored), nz), lax.rem(item, stored)),
+            lambda item: lax.div(item, stored * nz))
+    by_z = (lambda target: y * nz + target, lambda item: (lax.div(item, stored * nz), lax.rem(item, stored)),
+            lambda item: lax.rem(lax.div(item, stored), nz))
+
+    def gather_z(direct, table, at):
+        if direct:
+            return Spread(table, z, nz, z_at, gather_send.at[at], gather_recv.at[at])
+        return Gather(table, z, nz, z_peers, zs, gather_send.at[at], gather_recv.at[at])
+
+    def gather_y(direct, table, at):
+        if direct:
+            return Spread(table, y, ny, y_at, gather_send.at[at], gather_recv.at[at])
+        return Gather(table, y, ny, y_peers, ys, gather_send.at[at], gather_recv.at[at])
+
+    def slots_y(relay, table, lists, picks, slots, at):
+        if relay:
+            return Relay(table, lists, slots, y, ny, y_at, relay_send.at[at], relay_recv.at[at], *by_y)
+        ring = Slots(
+            lambda index: table[index], lists, picks, slots, y, ny, y_peers, ys, slot_send.at[at], slot_recv.at[at], *by_y
         )
-
-    def along_z(table, lists, picks, slots, at):
-        return Slots(
-            lambda index: table[index], lists, picks, slots, z, nz, z_peers, zs, slot_send.at[at], slot_recv.at[at],
-            lambda target: y * nz + target,
-            lambda item: (lax.div(item, stored * nz), lax.rem(item, stored)),
-            lambda item: lax.rem(lax.div(item, stored), nz),
+        ring.prepare()
+        return ring
+
+    def slots_z(relay, table, lists, picks, slots, at):
+        if relay:
+            return Relay(table, lists, slots, z, nz, z_at, relay_send.at[at], relay_recv.at[at], *by_z)
+        ring = Slots(
+            lambda index: table[index], lists, picks, slots, z, nz, z_peers, zs, slot_send.at[at], slot_recv.at[at], *by_z
         )
-
-    downs = along_y(down_tab, adapter_list, range(listed), down_slots, 0)
-    ups = along_z(up_tab, adapter_list, range(listed), up_slots, 1)
-    pages = [
-        ring
-        for part in range(2)
-        for ring in (
-            along_y(kpage_tab, page_list, range(part * half, part * half + half), kpage_slots.at[part], 2 + part),
-            along_z(vpage_tab, page_list, range(part * half, part * half + half), vpage_slots.at[part], 4 + part),
-        )
-    ]
+        ring.prepare()
+        return ring
+
+    flows = {
+        "D": [gather_z("D" in DIRECT, down_tab, 0)],
+        "U": [gather_y("U" in DIRECT, up_tab, 1)],
+        "K": [gather_z("K" in DIRECT, kpage_tab, 2)],
+        "V": [gather_y("V" in DIRECT, vpage_tab, 3)],
+    }
+    every = range(listed)
+
+    def make_slots():
+        flows["d"] = [slots_y("d" in DIRECT, down_tab, adapter_list, every, down_slots, 0)]
+        flows["u"] = [slots_z("u" in DIRECT, up_tab, adapter_list, every, up_slots, 1)]
+        flows["k"], flows["v"] = [], []
+        for part in range(2):
+            picks = range(part * half, part * half + half)
+            flows["k"].append(slots_y(False, kpage_tab, page_list, picks, kpage_slots.at[part], 2 + part))
+            flows["v"].append(slots_z(False, vpage_tab, page_list, picks, vpage_slots.at[part], 4 + part))
+
+    state = {name: 0 for name in "DUKVduvk"}
+
+    def advance(name, upto=None):
+        steps = max(flow.steps for flow in flows[name])
+        while state[name] < (steps if upto is None else min(upto, steps)):
+            for flow in flows[name]:
+                if state[name] < flow.steps:
+                    flow.forward(state[name])
+            state[name] += 1
 
     rows = tokens // PREV_PARTS
     prevs = []
@@ -255,102 +379,69 @@
             waiting.pop(0).start()
 
     pl.semaphore_wait(barrier, len(greeted))
-    for copy, gather in zip(own, gathers):
+    for copy, name in zip(own, "DUKV"):
         copy.wait()
-        gather.start()
+        flows[name][0].start()
     idprev.start()
-    some_prev(1)
-
-    for ring in [downs, ups] + pages:
-        ring.prepare()
+    make_slots()
     staged[0].wait()
     code_columns = as_columns(page_entry_ref[...] * listed + adapter_entry_ref[...])
     for c in range(chunks):
         code_ref[pl.ds(c, 1), :] = token_codes(ids_ref[pl.ds(c, 1), :], code_columns)
         key_ids[pl.ds(tokens + c * BLOCK, BLOCK), :] = as_columns(ids_ref[pl.ds(c, 1), :])
 
-    gsteps = max(g.steps for g in gathers)
-
-    def gather_step(which, s):
-        for gather in which:
-            if 0 <= s < gather.steps:
-                gather.forward(s)
-
-    def slot_step(which, s):
-        for ring in which:
-            if 0 <= s < ring.steps:
-                ring.forward(s)
-
-    for s in range(gsteps):
-        gather_step(gathers[:2], s)
-        gather_step(gathers[2:], s - 1)
-        some_prev(1)
-    downs.start()
-    ups.start()
-    gather_step(gathers[2:], gsteps - 1)
-    slot_step([downs], 0)
-    for ring in pages:
-        ring.start()
-    slot_step([ups], 0)
-    steps = max(downs.steps, ups.steps)
-    for s in range(1, steps):
-        slot_step([downs], s)
-        slot_step([ups], s)
-        if s + 1 < steps:
-            slot_step(pages, s - 1)
-        some_prev(2)
-    some_prev(len(waiting))
-    served = max(steps - 2, 0)
-
-    for k in range(listed):
-        down_all[k * rank:(k + 1) * rank, :] = downs.entry(k)
-    staged[1].wait()
-    partial = lax.dot_general(down_all[...], x_ref[...], NT, preferred_element_type=F32)
-    for c in range(chunks):
-        entry = lax.rem(code_ref[pl.ds(c, 1), :], listed)
-        total = jnp.zeros((rank, BLOCK), F32)
-        for k in range(listed):
-            total = jnp.where(entry == k, partial[k * rank:(k + 1) * rank, c * BLOCK:(c + 1) * BLOCK], total)
-        parts[c] = total
     each = chunks // 2
     mine = pl.ds(core * each, each)
     theirs = pl.ds((1 - core) * each, each)
     to_pair = remote(parts.at[theirs], from_pair, pair_send.at[0], pair_recv.at[0], pair)
-    to_pair.start()
-    to_pair.wait_recv()
-    half_sum[...] = parts[mine] + from_pair[...]
     to_x = [
         remote(half_sum, from_x.at[d], x_send.at[d], x_recv.at[d], peer) for d, peer in enumerate(x_peers)
     ]
-    for copy in to_x:
-        copy.start()
-
-    for k in range(listed):
-        up_all[k * rank:(k + 1) * rank, :] = ups.entry(k)
-    for copy in staged[2:]:
-        copy.wait()
-    for c in range(chunks):
-        at = tokens + c * BLOCK
-        values_t[:, at:at + BLOCK] = values[at:at + BLOCK, :].T
-    if served + 1 < steps:
-        slot_step(pages, served)
-        served += 1
-    for copy in prevs + [idprev]:
-        copy.wait_recv()
-    first = group == 0
-    for c in range(chunks):
-        at = c * BLOCK
-        values_t[:, at:at + BLOCK] = values[at:at + BLOCK, :].T
-        key_ids[at:at + BLOCK, :] = as_columns(jnp.where(first, -1, idprev_ref[pl.ds(c, 1), :]))
-
-    total = half_sum[...]
-    for d, copy in enumerate(to_x):
-        copy.wait_recv()
-        total = total + from_x[d]
-    lowrank_ref[mine] = total.astype(BF16)
     back = remote(lowrank_ref.at[mine], lowrank_ref.at[mine], pair_send.at[1], pair_recv.at[1], pair)
-    back.start()
-    back.wait_recv()
+
+    def project():
+        advance("d")
+        for k in range(listed):
+            down_all[k * rank:(k + 1) * rank, :] = flows["d"][0].entry(k)
+        staged[1].wait()
+        partial = lax.dot_general(down_all[...], x_ref[...], NT, preferred_element_type=F32)
+        for c in range(chunks):
+            entry = lax.rem(code_ref[pl.ds(c, 1), :], listed)
+            total = jnp.zeros((rank, BLOCK), F32)
+            for k in range(listed):
+                total = jnp.where(entry == k, partial[k * rank:(k + 1) * rank, c * BLOCK:(c + 1) * BLOCK], total)
+            parts[c] = total
+        to_pair.start()
+        to_pair.wait_recv()
+        half_sum[...] = parts[mine] + from_pair[...]
+        for copy in to_x:
+            copy.start()
+
+    def own_values():
+        for copy in staged[2:]:
+            copy.wait()
+        for c in range(chunks):
+            at = tokens + c * BLOCK
+            values_t[:, at:at + BLOCK] = values[at:at + BLOCK, :].T
+
+    def ready():
+        for copy in prevs + [idprev]:
+            copy.wait_recv()
+        first = group == 0
+        for c in range(chunks):
+            at = c * BLOCK
+            values_t[:, at:at + BLOCK] = values[at:at + BLOCK, :].T
+            key_ids[at:at + BLOCK, :] = as_columns(jnp.where(first, -1, idprev_ref[pl.ds(c, 1), :]))
+        advance("u")
+        for k in range(listed):
+            up_all[k * rank:(k + 1) * rank, :] = flows["u"][0].entry(k)
+        total = half_sum[...]
+        for d, copy in enumerate(to_x):
+            copy.wait_recv()
+            total = total + from_x[d]
+        lowrank_ref[mine] = total.astype(BF16)
+        back.start()
+        back.wait_recv()
 
     band = tokens + BLOCK
     later = lax.broadcasted_iota(jnp.int32, (BLOCK, BLOCK), 0)
@@ -386,17 +477,37 @@
         )
         return carry
 
-    while served + 1 < steps:
-        slot_step(pages, served)
-        served += 1
-    lax.fori_loop(0, chunks, band_block, 0, unroll=2)
-    slot_step(pages, served)
+    quarter = max(chunks // 4, 1)
+    turn = 0
+    for token in SCHEDULE:
+        name, what = token[0], token[1:]
+        if name in state:
+            if what == "*":
+                advance(name.upper())
+                for flow in flows[name]:
+                    flow.start()
+            else:
+                advance(name, int(what) + 1)
+        elif name == "p":
+            some_prev(int(what))
+        elif name == "P":
+            project()
+        elif name == "O":
+            own_values()
+        elif name == "R":
+            some_prev(len(waiting))
+            ready()
+        elif name == "B" and turn * quarter < chunks:
+            lax.fori_loop(turn * quarter, turn * quarter + quarter, band_block, 0, unroll=quarter)
+            turn += 1
+    advance("k")
+    advance("v")
 
     for part in range(2):
         for k in range(half):
             at = (part * half + k) * PAGE
-            kpages[at:at + PAGE, :] = pages[2 * part].entry(k)
-            vpages_t[:, at:at + PAGE] = pages[2 * part + 1].entry(k).T
+            kpages[at:at + PAGE, :] = flows["k"][part].entry(k)
+            vpages_t[:, at:at + PAGE] = flows["v"][part].entry(k).T
 
     def page_block(i, carry):
         start = pl.multiple_of(i * BLOCK, BLOCK)
@@ -431,8 +542,9 @@
 
     for copy in prevs + [idprev, to_pair, back] + to_x:
         copy.wait_send()
-    for ring in gathers + [downs, ups] + pages:
-        ring.finish()
+    for some in flows.values():
+        for flow in some:
+            flow.finish()
     for i in range(chunks):
         at = pl.ds(i * BLOCK, BLOCK)
         pltpu.make_async_copy(out_ref.at[at], out_hbm.at[at], done.at[i]).wait()
@@ -461,8 +573,8 @@
             pltpu.VMEM((ny, stored, rank, features), BF16),
             pltpu.VMEM((nz, stored, PAGE, HEAD_WIDTH), BF16),
             pltpu.VMEM((ny, stored, PAGE, HEAD_WIDTH), BF16),
-            pltpu.VMEM((ny + 1, listed, rank, features), BF16),
-            pltpu.VMEM((nz + 1, listed, rank, features), BF16),
+            pltpu.VMEM((max(3 * len(CHAINS[ny]), ny + 1), listed, rank, features), BF16),
+            pltpu.VMEM((max(3 * len(CHAINS[nz]), nz + 1), listed, rank, features), BF16),
             pltpu.VMEM((2, ny + 1, half, PAGE, HEAD_WIDTH), BF16),
             pltpu.VMEM((2, nz + 1, half, PAGE, HEAD_WIDTH), BF16),
             pltpu.VMEM(x.shape, BF16),
@@ -488,7 +600,7 @@
             pltpu.VMEM((chunks, 8, BLOCK), F32),
             pltpu.VMEM((chunks, HEAD_WIDTH, stack), F32),
             pltpu.VMEM(q.shape, BF16),
-            dma((4, most)), dma((4, most)), dma((6, most)), dma((6, most)),
+            dma((4, most)), dma((4, most)), dma((2, 4, 2)), dma((2, 4, 2)), dma((6, most)), dma((6, most)),
             dma((3, PREV_PARTS)), dma((3, PREV_PARTS)),
             dma((2,)), dma((2,)), dma((nx,)), dma((nx,)),
             dma((9,)), dma((chunks,)),

time: 78 us -> 73.9 us (0.947)
  the two profiles are of different devices: /device:TPU:1 before, /device:TPU:6 now
where the time goes in v3:
time: 73.9 us; the launch traced here: 73.7 us
  Pallas kernels  71.5 us (97%)
  local copies, waits for them, and re-layouts  2.26 us (3%)
    pallas_call x1, Pallas kernels, fused(): pl.pallas_call(functools.partial(fused_kernel, ny, nz, ntp), out_shape=ja...  71.5 us
    unnamed x1, local copies, waits for them, and re-layouts  2.26 us

profile of v3, /device:TPU:6, one launch (start us, length us, event | category | flops | bytes accessed | tf_op | source)
XLA Modules:
  0.0 73.7 jit_solution(14952947823245033184)
XLA Ops:
  0.0 71.5 %fused.1 = bf16[1024,512]{1,0:T(8,128)(2,1)} custom-call(s32[4,64]{1,0:T(4,128)} %bitcast.6, s32[4,64]{1,0:T(4,128)} %bitcast.7, s32[1,256]{1,0:T(1,128)} %bitcast.8, s32[1,256]{1,0:T(1,128)} %bitcast.9, s32[8,128]{1,0:T(8,128)} %bitcast.5, bf16[1024,512]{1,0:T(8,128)(2,1)} %x_hbm.1, bf16[1024,512]{1,0:T(8,128)(2,1)} %q_hbm.1, bf16[1024,128]{1,0:T(8,128)(2,1)} %k_hbm.1, ...), custom_call_target="tpu_custom_call" | custom-call | tf_op jit(solution)/shard_map/fused/pallas_call | solution.py:566
  71.5 2.3 %copy.14 = bf16[1024,512]{1,0:T(8,128)(2,1)} copy(bf16[1024,512]{1,0:T(8,128)(2,1)} %fused.1) | data formatting | bytes 2097152

commit v4 on v3

--- a/solution.py
+++ b/solution.py
@@ -232,6 +232,7 @@
 
 
 PREV_PARTS = 4
+PAGE_UNROLL = 4
 DIRECT = "du"
 SCHEDULE = (
     "D0", "U0", "K0", "V0", "p1", "D1", "U1", "K1", "V1", "p1", "D2", "U2",
@@ -538,7 +539,7 @@
         pltpu.make_async_copy(out_ref.at[at], out_hbm.at[at], done.at[i]).start()
         return carry
 
-    lax.fori_loop(0, chunks, page_block, 0, unroll=2)
+    lax.fori_loop(0, chunks, page_block, 0, unroll=min(chunks, PAGE_UNROLL))
 
     for copy in prevs + [idprev, to_pair, back] + to_x:
         copy.wait_send()

time: 73.9 us -> 73.5 us (level)
  no operation moved by 1% of the time
where the time goes in v4:
time: 73.5 us; the launch traced here: 73.3 us
  Pallas kernels  71 us (97%)
  local copies, waits for them, and re-layouts  2.26 us (3%)
    pallas_call x1, Pallas kernels, fused(): pl.pallas_call(functools.partial(fused_kernel, ny, nz, ntp), out_shape=ja...  71 us
    unnamed x1, local copies, waits for them, and re-layouts  2.26 us

profile of v4, /device:TPU:6, one launch (start us, length us, event | category | flops | bytes accessed | tf_op | source)
XLA Modules:
  0.0 73.3 jit_solution(3920333447722696284)
XLA Ops:
  0.0 71.0 %fused.1 = bf16[1024,512]{1,0:T(8,128)(2,1)} custom-call(s32[4,64]{1,0:T(4,128)} %bitcast.6, s32[4,64]{1,0:T(4,128)} %bitcast.7, s32[1,256]{1,0:T(1,128)} %bitcast.8, s32[1,256]{1,0:T(1,128)} %bitcast.9, s32[8,128]{1,0:T(8,128)} %bitcast.5, bf16[1024,512]{1,0:T(8,128)(2,1)} %x_hbm.1, bf16[1024,512]{1,0:T(8,128)(2,1)} %q_hbm.1, bf16[1024,128]{1,0:T(8,128)(2,1)} %k_hbm.1, ...), custom_call_target="tpu_custom_call" | custom-call | tf_op jit(solution)/shard_map/fused/pallas_call | solution.py:567
  71.0 2.3 %copy.14 = bf16[1024,512]{1,0:T(8,128)(2,1)} copy(bf16[1024,512]{1,0:T(8,128)(2,1)} %fused.1) | data formatting | bytes 2097152

commit v5 on v4

--- a/solution.py
+++ b/solution.py
@@ -164,9 +164,11 @@
 
 
 class Relay:
-    def __init__(self, table, lists, slots, pos, n, peer_at, send, recv, group_at, index_of, place_of):
+    def __init__(self, table, lists, slots, pos, n, peer_at, send, recv, group_at, index_of, place_of, mirror=False):
         self.table, self.slots, self.pos, self.n = table, slots, pos, n
         self.chains = CHAINS[n]
+        if mirror and n > 2:
+            self.chains = tuple(tuple(-offset for offset in chain) for chain in self.chains)
         self.plan, self.first, self.second = {}, [], []
         count = lists.shape[0]
         targets = [0] + [-offset for chain in self.chains for offset in chain]
@@ -332,7 +334,7 @@
 
     def slots_z(relay, table, lists, picks, slots, at):
         if relay:
-            return Relay(table, lists, slots, z, nz, z_at, relay_send.at[at], relay_recv.at[at], *by_z)
+            return Relay(table, lists, slots, z, nz, z_at, relay_send.at[at], relay_recv.at[at], *by_z, mirror=True)
         ring = Slots(
             lambda index: table[index], lists, picks, slots, z, nz, z_peers, zs, slot_send.at[at], slot_recv.at[at], *by_z
         )

time: 73.5 us -> 73.5 us (level)
  no operation moved by 1% of the time
where the time goes in v5:
time: 73.5 us; the launch traced here: 73.3 us
  Pallas kernels  71 us (97%)
  local copies, waits for them, and re-layouts  2.26 us (3%)
    pallas_call x1, Pallas kernels, fused(): pl.pallas_call(functools.partial(fused_kernel, ny, nz, ntp), out_shape=ja...  71 us
    unnamed x1, local copies, waits for them, and re-layouts  2.26 us

profile of v5, /device:TPU:6, one launch (start us, length us, event | category | flops | bytes accessed | tf_op | source)
XLA Modules:
  0.0 73.3 jit_solution(17782881049703187962)
XLA Ops:
  0.0 71.0 %fused.1 = bf16[1024,512]{1,0:T(8,128)(2,1)} custom-call(s32[4,64]{1,0:T(4,128)} %bitcast.6, s32[4,64]{1,0:T(4,128)} %bitcast.7, s32[1,256]{1,0:T(1,128)} %bitcast.8, s32[1,256]{1,0:T(1,128)} %bitcast.9, s32[8,128]{1,0:T(8,128)} %bitcast.5, bf16[1024,512]{1,0:T(8,128)(2,1)} %x_hbm.1, bf16[1024,512]{1,0:T(8,128)(2,1)} %q_hbm.1, bf16[1024,128]{1,0:T(8,128)(2,1)} %k_hbm.1, ...), custom_call_target="tpu_custom_call" | custom-call | tf_op jit(solution)/shard_map/fused/pallas_call | solution.py:569
  71.0 2.3 %copy.14 = bf16[1024,512]{1,0:T(8,128)(2,1)} copy(bf16[1024,512]{1,0:T(8,128)(2,1)} %fused.1) | data formatting | bytes 2097152
